TPU v7x, 256 devices: a whole 4x4x8 slice. The times are simulated.
256 devices in a mesh: freq: 64 (over y, z, core), sky: 4 (over x).
Axes of the slice: x: 4, y: 4, z: 8, core: 2. Of those that a mesh axis runs over, the one named last changes fastest.
Arguments:
- sky_maps: bfloat16 [1024, 96, 4096], P('freq', 'sky'), may hold values from -240 to 240
- beam_index: int32 [1024], P('freq'), may hold values from 0 to 7
- beam_taps: float32 [8, 31], replicated, may hold values from 0.05 to 1
- start_seed: int32 [1024, 16], replicated, may hold values from -64 to 64
Outputs:
- cleaned: bfloat16 [1024, 256, 1536], P(None, ('freq', 'sky'))
All inputs are finite; a program needn't handle non-finite values.
Results may differ from a plain program's by a relative error of at most 0.0079.
The roundings to bfloat16 on the way count: a program that leaves them out, or rounds other values in their place, can miss the bound.
Values may be sent and summed in bfloat16 or wider, within the bound.
No kernel may reach another device: no remote copies, remote signals or barrier semaphores. Data moves between devices by JAX's collectives and lax.ppermute only.
A program may use at most 64 MiB of HBM per device.

v0:
```python
import jax
import jax.numpy as jnp
from jax import lax
from jax.sharding import PartitionSpec as P

ITERS = 8


def with_halo(x, sides, width):
    for axis, dim in sides:
        size, length = (lax.axis_size(axis), x.shape[dim])
        up = [(i, (i + 1) % size) for i in range(size - 1)]
        down = [(j, i) for i, j in up]
        last = lax.slice_in_dim(x, length - width, length, axis=dim)
        leading = lax.slice_in_dim(x, 0, width, axis=dim)
        before = lax.ppermute(last, axis, up)
        after = lax.ppermute(leading, axis, down)
        x = jnp.concatenate([before, x, after], axis=dim)
    return x


def column_pass(padded, kernels, strip_rows, half_taps, tap_count):
    row_pass = jnp.zeros((padded.shape[0], strip_rows, padded.shape[2]), jnp.float32)
    for offset in range(tap_count):
        row_pass = row_pass + kernels[:, offset, None, None] * padded[
            :, offset : offset + strip_rows, :
        ].astype(jnp.float32)
    columns = padded.shape[2]
    widened = jnp.pad(row_pass, ((0, 0), (0, 0), (half_taps, half_taps)))
    col_pass = jnp.zeros(row_pass.shape, jnp.float32)
    for offset in range(tap_count):
        col_pass = (
            col_pass + kernels[:, offset, None, None] * widened[:, :, offset : offset + columns]
        )
    return col_pass.astype(jnp.bfloat16)


def orthonormal(images):
    gram_matrix = jnp.dot(images.T, images, precision=lax.Precision.HIGHEST)
    factor = jnp.linalg.cholesky(gram_matrix)
    return lax.linalg.triangular_solve(
        factor, images, left_side=False, lower=True, transpose_a=True
    )


def local_covariance(tile_data):
    return lax.dot_general(
        tile_data, tile_data, (((1,), (1,)), ((), ())), preferred_element_type=jnp.float32
    )


def body(sky_maps, beam_index, beam_taps, start_seed):
    channels, strip_rows, columns = sky_maps.shape
    beam_count, tap_count = beam_taps.shape
    half_taps = (tap_count - 1) // 2
    onehot = (beam_index[:, None] == jnp.arange(beam_count, dtype=jnp.int32)[None, :]).astype(
        jnp.float32
    )
    tap_rows = jnp.dot(onehot, beam_taps, precision=lax.Precision.HIGHEST)
    kernels = tap_rows / jnp.sum(tap_rows, axis=1, keepdims=True)
    padded = with_halo(sky_maps, (("sky", 1),), half_taps)
    smoothed = column_pass(padded, kernels, strip_rows, half_taps, tap_count)
    freq_count = lax.axis_size("freq")
    sky_count = lax.axis_size("sky")
    tile_cols = columns // freq_count
    grouped = lax.all_to_all(
        smoothed.reshape(channels, strip_rows, freq_count, tile_cols),
        "freq",
        split_axis=2,
        concat_axis=0,
        tiled=True,
    )
    all_chans = channels * freq_count
    tile_data = grouped.reshape(all_chans, strip_rows * tile_cols)
    wide_tile = tile_data.astype(jnp.float32)
    total_pixels = strip_rows * columns * sky_count
    subspace = start_seed.astype(jnp.float32)
    covariance = lax.psum(local_covariance(tile_data), ("freq", "sky")) / total_pixels
    for sweep in range(ITERS):
        images = jnp.dot(covariance, subspace, precision=lax.Precision.HIGHEST)
        subspace = orthonormal(images)
    coeffs = jnp.dot(subspace.T, wide_tile, precision=lax.Precision.HIGHEST)
    cleaned = (wide_tile - jnp.dot(subspace, coeffs, precision=lax.Precision.HIGHEST)).astype(
        jnp.bfloat16
    )
    return cleaned.reshape(all_chans, 1, strip_rows * tile_cols)


def solution(mesh):
    return jax.shard_map(
        body,
        mesh=mesh,
        in_specs=(P("freq", "sky", None), P("freq"), P(), P()),
        out_specs=P(None, ("freq", "sky"), None),
        check_vma=False,
    )
```

profile of v0, /device:TPU:2, one launch (start us, length us, event | category | flops | bytes accessed | tf_op | source)
XLA Modules:
  0.0 664.6 jit_solution(16235698417459183960)
XLA Ops:
  6.5 2.9 fusion.109
  9.5 1.2 copy.36
  10.7 3.4 collective-permute-start
  14.1 1.2 copy.37
  15.2 2.6 collective-permute-start.1
  18.6 0.5 slice_reduce_fusion.30
  19.4 37.7 %collective-permute-done = bf16[16,15,4096]{2,0,1:T(8,128)(2,1)S(1)} collective-permute-done((bf16[16,15,4096]{2,0,1:T(8,128)(2,1)S(1)}, bf16[16,15,4096]{2,0,1:T(8,128)(2,1)S(1)}, u32[]{:S(2)}, u32[]{:S(2)}) %collective-permute-start) | collective-permute-done | bytes 1966112 | tf_op jit(solution)/shard_map/ppermute | solution.py:16
  57.1 1.1 copy.24
  58.2 3.2 collective-permute-done.1
  61.4 1.1 copy_dynamic-update-slice_fusion
  62.5 40.9 %multiply_add_fusion = f32[16,24,4096]{2,1,0:T(8,128)S(1)} fusion(bf16[16,24,4096]{2,1,0:T(8,128)(2,1)S(1)} %copy-done.2, bf16[16,15,4096]{2,1,0:T(8,128)(2,1)S(1)} %copy.24, bf16[16,39,4096]{2,1,0:T(8,128)(2,1)S(1)} %copy_dynamic-update-slice_fusion, f32[16]{0:T(128)S(1)} %get-tuple-element.8, f32[16]{0:T(128)S(1)} %get-tuple-element.9, ...), kind=kLoop, calls=%fused_computation.62 | loop fusion | flops 215482368 | bytes 58591168 | tf_op jit(solution)/shard_map/add | solution.py:25
  103.4 50.4 %add_convert_fusion = bf16[16,24,4096]{2,1,0:T(8,128)(2,1)S(1)} fusion(f32[16,24,4096]{2,1,0:T(8,128)S(1)} %multiply_add_fusion, f32[16]{0:T(128)S(1)} %get-tuple-element.8, f32[16]{0:T(128)S(1)} %get-tuple-element.9, f32[16]{0:T(128)S(1)} %get-tuple-element.10, f32[16]{0:T(128)S(1)} %get-tuple-element.11, f32[16]{0:T(128)S(1)} %get-tuple-element.12, ...), kind=kLoop, calls=%fused_computation.29 | loop fusion | flops 97517568 | bytes 9439168 | tf_op jit(solution)/shard_map/convert_element_type | solution.py:35
  153.8 7.9 %reshape.54 = bf16[16,24,64,64]{3,2,1,0:T(8,128)(2,1)} reshape(bf16[16,24,4096]{2,1,0:T(8,128)(2,1)S(1)} %add_convert_fusion) | data formatting | bytes 6291456 | tf_op jit(solution)/shard_map/reshape | solution.py:67
  161.7 9.5 %copy.40 = bf16[16,24,64,64]{3,1,0,2:T(8,128)(2,1)} copy(bf16[16,24,64,64]{3,2,1,0:T(8,128)(2,1)} %reshape.54) | data formatting | bytes 6291456 | tf_op jit(solution)/shard_map/reshape | solution.py:67
  171.2 9.7 %reshape.118 = bf16[64,2,12288]{2,1,0:T(2,128)(2,1)S(1)} reshape(bf16[64,16,24,64]{3,2,1,0:T(8,128)(2,1)} %bitcast.141) | data formatting | bytes 6291456
  180.9 85.0 %all_to_all.15 = bf16[64,2,12288]{2,1,0:T(2,128)(2,1)} all-to-all(bf16[64,2,12288]{2,1,0:T(2,128)(2,1)S(1)} %reshape.118), channel_id=1, replica_groups=mesh['freq'=64,'sky'=4] {'freq'}, dimensions={0} | all-to-all | bytes 6291456 | tf_op jit(solution)/shard_map/all_to_all | solution.py:66
  265.9 11.1 %reshape.119 = bf16[64,16,24,64]{3,2,1,0:T(8,128)(2,1)} reshape(bf16[64,2,12288]{2,1,0:T(2,128)(2,1)} %all_to_all.15) | data formatting | bytes 6291456
  277.0 7.4 %bitcast_bitcast_fusion = bf16[64,16,24,1,64]{4,2,1,0,3:T(8,128)(2,1)} fusion(bf16[64,16,24,64]{3,2,1,0:T(8,128)(2,1)} %reshape.119), kind=kLoop, calls=%fused_computation.224 | loop fusion | bytes 6291456 | tf_op jit(solution)/shard_map/all_to_all | solution.py:66
  284.5 7.9 %reshape.55 = bf16[1024,1536]{1,0:T(8,128)(2,1)S(1)} reshape(bf16[64,16,24,1,64]{4,2,1,0,3:T(8,128)(2,1)} %bitcast_bitcast_fusion) | data formatting | bytes 6291456 | tf_op jit(solution)/shard_map/reshape | solution.py:74
  292.4 5.4 fusion.111
  297.8 267.5 %all-reduce.3.cloned.1.call-done = f32[1024,1024]{1,0:T(8,128)} async-done(((f32[1024,1024]{1,0:T(8,128)}), f32[1024,1024]{1,0:T(8,128)}) %all-reduce.3.cloned.1.call-update) | async-done | bytes 4194320 | tf_op jit(solution)/shard_map/psum | solution.py:78
  565.3 5.9 fusion.50
  571.5 1.5 cholesky.134
  573.0 0.6 compare_reduce_fusion.7
  573.7 0.6 fusion.61
  574.3 1.2 custom-call.12
  575.8 5.9 fusion.48
  582.0 1.5 cholesky.145
  583.5 0.6 compare_reduce_fusion.6
  584.1 0.6 fusion.62
  584.8 1.2 custom-call.13
  586.3 5.9 fusion.46
  592.5 1.5 cholesky.156
  594.0 0.6 compare_reduce_fusion.5
  594.6 0.6 fusion.63
  595.3 1.2 custom-call.14
  596.8 5.9 fusion.44
  602.9 1.6 cholesky.167
  604.6 0.6 compare_reduce_fusion.4
  605.3 0.6 fusion.64
  605.9 1.2 custom-call.15
  607.4 5.9 fusion.42
  613.6 1.5 cholesky.178
  615.1 0.6 compare_reduce_fusion.3
  615.7 0.6 fusion.65
  616.4 1.2 custom-call.16
  617.9 5.9 fusion.40
  624.1 1.5 cholesky.189
  625.6 0.6 compare_reduce_fusion.2
  626.2 0.6 fusion.66
  626.9 1.2 custom-call.17
  628.4 5.9 fusion.38
  634.5 1.5 cholesky.200
  636.1 0.6 compare_reduce_fusion.1
  636.7 0.6 fusion.67
  637.4 1.2 custom-call.18
  638.9 5.9 fusion.36
  644.7 0.4 fusion.119
  645.2 1.5 cholesky.211
  646.8 0.6 compare_reduce_fusion
  647.4 0.6 fusion.68
  648.1 1.2 custom-call.19
  649.6 1.3 fusion.120
  650.9 6.7 %fusion.21 = bf16[1024,1,1536]{2,0,1:T(8,128)(2,1)} fusion(f32[1024,16]{0,1:T(8,128)S(1)} %convolution_bitcast_fusion, f32[16,1536]{1,0:T(8,128)S(1)} %fusion.120, bf16[1024,1536]{1,0:T(8,128)(2,1)S(1)} %reshape.55), kind=kOutput, calls=%fused_computation.63 | convolution fusion | flops 306708480 | bytes 6455296 | tf_op jit(solution)/shard_map/dot_general | solution.py:83
  (55 shorter events, 5.6 us)
Async XLA Ops:
  6.5 11.3 %copy-start = (f32[8,31]{1,0:T(8,128)S(1)}, f32[8,31]{1,0:T(8,128)}, u32[]{:S(2)}) copy-start(f32[8,31]{1,0:T(8,128)} %param.9) | copy-start | bytes 2980
  6.5 11.3 %copy-start.4 = (s32[16]{0:T(128)S(1)}, s32[16]{0:T(128)}, u32[]{:S(2)}) copy-start(s32[16]{0:T(128)} %param.8) | copy-start | bytes 196
  6.5 558.8 %all-reduce.3.cloned.1.call-start = ((), (), s32[]{:S(2)}) async-start(), calls=%async_computation.1 | async-start | bytes 8388608 | tf_op jit(solution)/shard_map/psum | solution.py:78
  9.5 9.6 %copy-start.2 = (bf16[16,24,4096]{2,1,0:T(8,128)(2,1)S(1)}, bf16[16,24,4096]{2,1,0:T(8,128)(2,1)}, u32[]{:S(2)}) copy-start(bf16[16,24,4096]{2,1,0:T(8,128)(2,1)} %param.7) | copy-start | bytes 9437188
  10.7 46.5 %collective-permute-start = (bf16[16,15,4096]{2,0,1:T(8,128)(2,1)S(1)}, bf16[16,15,4096]{2,0,1:T(8,128)(2,1)S(1)}, u32[]{:S(2)}, u32[]{:S(2)}) collective-permute-start(bf16[16,15,4096]{2,0,1:T(8,128)(2,1)S(1)} %copy.36), channel_id=1, source_target_pairs={{0,1},{1,2},{2,3},{4,5},{5,6},{6,7},{8,9},{9,10},{10,11},{12,13},{... | collective-permute-start | bytes 5898248 | tf_op jit(solution)/shard_map/ppermute | solution.py:16
  15.2 46.2 %collective-permute-start.1 = (bf16[16,15,4096]{2,0,1:T(8,128)(2,1)S(1)}, bf16[16,15,4096]{2,0,1:T(8,128)(2,1)S(1)}, u32[]{:S(2)}, u32[]{:S(2)}) collective-permute-start(bf16[16,15,4096]{2,0,1:T(8,128)(2,1)S(1)} %copy.37), channel_id=1, source_target_pairs={{1,0},{2,1},{3,2},{5,4},{6,5},{7,6},{9,8},{10,9},{11,10},{13,12},{... | collective-permute-start | bytes 5898248 | tf_op jit(solution)/shard_map/ppermute | solution.py:17
  292.4 273.0 %copy-start.3 = (s32[1024,16]{0,1:T(8,128)S(1)}, s32[1024,16]{0,1:T(8,128)}, u32[]{:S(2)}) copy-start(s32[1024,16]{0,1:T(8,128)} %param.10) | copy-start | bytes 196612
  638.6 18.9 %copy-start.1 = (f32[8,31]{1,0:T(8,128)S(1)}, f32[8,31]{1,0:T(8,128)}, u32[]{:S(2)}) copy-start(f32[8,31]{1,0:T(8,128)} %param.9) | copy-start | bytes 2980
Sparse Core Ops, SparseCore 0:
  297.9 267.3 all-reduce.2
where the time goes:
time: 671 us; the launch traced here: 665 us
  waiting for transfers between devices  308 us (46%)
  other arithmetic  124 us (18%)
  blocking collectives  85 us (13%)
  matrix products  64.5 us (10%)
  local copies, waits for them, and re-layouts  62.9 us (9%)
  between operations  13.9 us (2%)
    psum x1, waiting for transfers between devices, body(): lax.psum(local_covariance(tile_data), ('freq', 'sky')) / total_pixels  268 us
    all_to_all x1, blocking collectives, body(): lax.all_to_all(smoothed.reshape(channels, strip_rows, freq_count, tile_co...  85 us
    convert_element_type x1, other arithmetic, column_pass(): return col_pass.astype(jnp.bfloat16)  50.4 us
    dot_general x8, matrix products, body(): images = jnp.dot(covariance, subspace, precision=lax.Precision.HIGHEST)  47 us
    add x1, other arithmetic, column_pass(): row_pass + kernels[:, offset, None, None] * padded[:, offset:offset + str...  40.9 us
    ppermute x1, waiting for transfers between devices, with_halo(): before = lax.ppermute(last, axis, up)  37.7 us
    unnamed x15, local copies, waits for them, and re-layouts  23.5 us
    another operation x24, other arithmetic, orthonormal(): factor = jnp.linalg.cholesky(gram_matrix)  17.5 us
  transfers between devices with their start and end apart: 3, of which 3 were waited for; matrix products, arithmetic and copies ran while one was open for 1% of the time, Pallas kernels for 0%

commit v1 on v0

--- a/solution.py
+++ b/solution.py
@@ -4,6 +4,12 @@
 from jax.sharding import PartitionSpec as P
 
 ITERS = 8
+
+
+def wait_desk_all(raw, device_axis, mesh_name):
+    for it in (device_axis, mesh_name):
+        raw = lax.psum(raw, axis_name=it)
+    return raw
 
 
 def with_halo(x, sides, width):
@@ -75,7 +81,7 @@
     wide_tile = tile_data.astype(jnp.float32)
     total_pixels = strip_rows * columns * sky_count
     subspace = start_seed.astype(jnp.float32)
-    covariance = lax.psum(local_covariance(tile_data), ("freq", "sky")) / total_pixels
+    covariance = wait_desk_all(local_covariance(tile_data), "freq", "sky") / total_pixels
     for sweep in range(ITERS):
         images = jnp.dot(covariance, subspace, precision=lax.Precision.HIGHEST)
         subspace = orthonormal(images)

time: 671 us -> 696 us (1.037)
  waiting for transfers between devices: 308 us -> 332 us
    psum x1 -> x2, waiting for transfers between devices: 268 us -> 291 us  [wait_desk_all(): raw = lax.psum(raw, axis_name=it)]
  transfers between devices with their start and end apart: 3 -> 4, of which waited for: 3 -> 4; matrix products, arithmetic and copies ran while one was open for 1% -> 1% of each run, Pallas kernels for 0% -> 0%
where the time goes in v1:
time: 696 us; the launch traced here: 688 us
  waiting for transfers between devices  332 us (48%)
  other arithmetic  124 us (18%)
  blocking collectives  85 us (12%)
  matrix products  64.1 us (9%)
  local copies, waits for them, and re-layouts  62.9 us (9%)
  between operations  13.9 us (2%)
    psum x2, waiting for transfers between devices, wait_desk_all(): raw = lax.psum(raw, axis_name=it)  291 us
    all_to_all x1, blocking collectives, body(): lax.all_to_all(smoothed.reshape(channels, strip_rows, freq_count, tile_co...  85 us
    convert_element_type x1, other arithmetic, column_pass(): return col_pass.astype(jnp.bfloat16)  50.4 us
    dot_general x8, matrix products, body(): images = jnp.dot(covariance, subspace, precision=lax.Precision.HIGHEST)  47.2 us
    add x1, other arithmetic, column_pass(): row_pass + kernels[:, offset, None, None] * padded[:, offset:offset + str...  40.9 us
    ppermute x1, waiting for transfers between devices, with_halo(): before = lax.ppermute(last, axis, up)  37.7 us
    unnamed x15, local copies, waits for them, and re-layouts  23.5 us
    another operation x24, other arithmetic, orthonormal(): factor = jnp.linalg.cholesky(gram_matrix)  17.5 us
  transfers between devices with their start and end apart: 4, of which 4 were waited for; matrix products, arithmetic and copies ran while one was open for 1% of the time, Pallas kernels for 0%

profile of v1, /device:TPU:2, one launch (start us, length us, event | category | flops | bytes accessed | tf_op | source)
XLA Modules:
  0.0 688.2 jit_solution(17326800613658973548)
XLA Ops:
  6.5 2.9 fusion.109
  9.5 1.2 copy.36
  10.7 3.4 collective-permute-start
  14.1 1.2 copy.37
  15.2 2.6 collective-permute-start.1
  18.6 0.5 slice_reduce_fusion.30
  19.4 37.7 %collective-permute-done = bf16[16,15,4096]{2,0,1:T(8,128)(2,1)S(1)} collective-permute-done((bf16[16,15,4096]{2,0,1:T(8,128)(2,1)S(1)}, bf16[16,15,4096]{2,0,1:T(8,128)(2,1)S(1)}, u32[]{:S(2)}, u32[]{:S(2)}) %collective-permute-start) | collective-permute-done | bytes 1966112 | tf_op jit(solution)/shard_map/ppermute | solution.py:22
  57.1 1.1 copy.24
  58.2 3.2 collective-permute-done.1
  61.4 1.1 copy_dynamic-update-slice_fusion
  62.5 40.9 %multiply_add_fusion = f32[16,24,4096]{2,1,0:T(8,128)S(1)} fusion(bf16[16,24,4096]{2,1,0:T(8,128)(2,1)S(1)} %copy-done.2, bf16[16,15,4096]{2,1,0:T(8,128)(2,1)S(1)} %copy.24, bf16[16,39,4096]{2,1,0:T(8,128)(2,1)S(1)} %copy_dynamic-update-slice_fusion, f32[16]{0:T(128)S(1)} %get-tuple-element.8, f32[16]{0:T(128)S(1)} %get-tuple-element.9, ...), kind=kLoop, calls=%fused_computation.62 | loop fusion | flops 215482368 | bytes 58591168 | tf_op jit(solution)/shard_map/add | solution.py:31
  103.4 50.4 %add_convert_fusion = bf16[16,24,4096]{2,1,0:T(8,128)(2,1)S(1)} fusion(f32[16,24,4096]{2,1,0:T(8,128)S(1)} %multiply_add_fusion, f32[16]{0:T(128)S(1)} %get-tuple-element.8, f32[16]{0:T(128)S(1)} %get-tuple-element.9, f32[16]{0:T(128)S(1)} %get-tuple-element.10, f32[16]{0:T(128)S(1)} %get-tuple-element.11, f32[16]{0:T(128)S(1)} %get-tuple-element.12, ...), kind=kLoop, calls=%fused_computation.29 | loop fusion | flops 97517568 | bytes 9439168 | tf_op jit(solution)/shard_map/convert_element_type | solution.py:41
  153.8 7.9 %reshape.54 = bf16[16,24,64,64]{3,2,1,0:T(8,128)(2,1)} reshape(bf16[16,24,4096]{2,1,0:T(8,128)(2,1)S(1)} %add_convert_fusion) | data formatting | bytes 6291456 | tf_op jit(solution)/shard_map/reshape | solution.py:73
  161.7 9.5 %copy.40 = bf16[16,24,64,64]{3,1,0,2:T(8,128)(2,1)} copy(bf16[16,24,64,64]{3,2,1,0:T(8,128)(2,1)} %reshape.54) | data formatting | bytes 6291456 | tf_op jit(solution)/shard_map/reshape | solution.py:73
  171.2 9.7 %reshape.118 = bf16[64,2,12288]{2,1,0:T(2,128)(2,1)S(1)} reshape(bf16[64,16,24,64]{3,2,1,0:T(8,128)(2,1)} %bitcast.141) | data formatting | bytes 6291456
  180.9 85.0 %all_to_all.15 = bf16[64,2,12288]{2,1,0:T(2,128)(2,1)} all-to-all(bf16[64,2,12288]{2,1,0:T(2,128)(2,1)S(1)} %reshape.118), channel_id=1, replica_groups=mesh['freq'=64,'sky'=4] {'freq'}, dimensions={0} | all-to-all | bytes 6291456 | tf_op jit(solution)/shard_map/all_to_all | solution.py:72
  265.9 11.1 %reshape.119 = bf16[64,16,24,64]{3,2,1,0:T(8,128)(2,1)} reshape(bf16[64,2,12288]{2,1,0:T(2,128)(2,1)} %all_to_all.15) | data formatting | bytes 6291456
  277.0 7.4 %bitcast_bitcast_fusion = bf16[64,16,24,1,64]{4,2,1,0,3:T(8,128)(2,1)} fusion(bf16[64,16,24,64]{3,2,1,0:T(8,128)(2,1)} %reshape.119), kind=kLoop, calls=%fused_computation.224 | loop fusion | bytes 6291456 | tf_op jit(solution)/shard_map/all_to_all | solution.py:72
  284.5 7.9 %reshape.55 = bf16[1024,1536]{1,0:T(8,128)(2,1)S(1)} reshape(bf16[64,16,24,1,64]{4,2,1,0,3:T(8,128)(2,1)} %bitcast_bitcast_fusion) | data formatting | bytes 6291456 | tf_op jit(solution)/shard_map/reshape | solution.py:80
  292.4 5.0 fusion.111
  297.9 193.1 %all-reduce.4.cloned.1.call-done = f32[1024,1024]{1,0:T(8,128)} async-done(((f32[1024,1024]{1,0:T(8,128)}), f32[1024,1024]{1,0:T(8,128)}) %all-reduce.4.cloned.1.call-update) | async-done | bytes 4194320 | tf_op jit(solution)/shard_map/psum | solution.py:11
  491.1 97.9 %all-reduce.6.cloned.1.call-done = f32[1024,1024]{1,0:T(8,128)} async-done(((f32[1024,1024]{1,0:T(8,128)}), f32[1024,1024]{1,0:T(8,128)}) %all-reduce.6.cloned.1.call-update) | async-done | bytes 4194320 | tf_op jit(solution)/shard_map/psum | solution.py:11
  589.0 5.9 fusion.50
  595.1 1.5 cholesky.134
  596.7 0.6 compare_reduce_fusion.7
  597.3 0.6 fusion.61
  598.0 1.2 custom-call.12
  599.5 5.9 fusion.48
  605.6 1.5 cholesky.145
  607.1 0.6 compare_reduce_fusion.6
  607.8 0.6 fusion.62
  608.5 1.2 custom-call.13
  610.0 5.9 fusion.46
  616.1 1.5 cholesky.156
  617.6 0.6 compare_reduce_fusion.5
  618.3 0.6 fusion.63
  618.9 1.2 custom-call.14
  620.4 5.9 fusion.44
  626.6 1.6 cholesky.167
  628.3 0.6 compare_reduce_fusion.4
  628.9 0.6 fusion.64
  629.6 1.2 custom-call.15
  631.1 5.9 fusion.42
  637.2 1.5 cholesky.178
  638.7 0.6 compare_reduce_fusion.3
  639.4 0.6 fusion.65
  640.0 1.2 custom-call.16
  641.6 5.9 fusion.40
  647.7 1.5 cholesky.189
  649.2 0.6 compare_reduce_fusion.2
  649.9 0.6 fusion.66
  650.5 1.2 custom-call.17
  652.0 5.9 fusion.38
  658.2 1.5 cholesky.200
  659.7 0.6 compare_reduce_fusion.1
  660.4 0.6 fusion.67
  661.0 1.2 custom-call.18
  662.5 6.1 fusion.36
  668.9 1.5 cholesky.211
  670.4 0.6 compare_reduce_fusion
  671.0 0.6 fusion.68
  671.7 1.2 custom-call.19
  673.2 1.3 fusion.120
  674.5 6.7 fusion.21
  (58 shorter events, 6.2 us)
Async XLA Ops:
  6.5 11.3 %copy-start = (f32[8,31]{1,0:T(8,128)S(1)}, f32[8,31]{1,0:T(8,128)}, u32[]{:S(2)}) copy-start(f32[8,31]{1,0:T(8,128)} %param.9) | copy-start | bytes 2980
  6.5 11.3 %copy-start.4 = (s32[16]{0:T(128)S(1)}, s32[16]{0:T(128)}, u32[]{:S(2)}) copy-start(s32[16]{0:T(128)} %param.8) | copy-start | bytes 196
  6.5 484.5 %all-reduce.4.cloned.1.call-start = ((), (), s32[]{:S(2)}) async-start(), calls=%async_computation.1 | async-start | bytes 8388608 | tf_op jit(solution)/shard_map/psum | solution.py:11
  9.5 9.6 %copy-start.2 = (bf16[16,24,4096]{2,1,0:T(8,128)(2,1)S(1)}, bf16[16,24,4096]{2,1,0:T(8,128)(2,1)}, u32[]{:S(2)}) copy-start(bf16[16,24,4096]{2,1,0:T(8,128)(2,1)} %param.7) | copy-start | bytes 9437188
  10.7 46.5 %collective-permute-start = (bf16[16,15,4096]{2,0,1:T(8,128)(2,1)S(1)}, bf16[16,15,4096]{2,0,1:T(8,128)(2,1)S(1)}, u32[]{:S(2)}, u32[]{:S(2)}) collective-permute-start(bf16[16,15,4096]{2,0,1:T(8,128)(2,1)S(1)} %copy.36), channel_id=1, source_target_pairs={{0,1},{1,2},{2,3},{4,5},{5,6},{6,7},{8,9},{9,10},{10,11},{12,13},{... | collective-permute-start | bytes 5898248 | tf_op jit(solution)/shard_map/ppermute | solution.py:22
  15.2 46.2 %collective-permute-start.1 = (bf16[16,15,4096]{2,0,1:T(8,128)(2,1)S(1)}, bf16[16,15,4096]{2,0,1:T(8,128)(2,1)S(1)}, u32[]{:S(2)}, u32[]{:S(2)}) collective-permute-start(bf16[16,15,4096]{2,0,1:T(8,128)(2,1)S(1)} %copy.37), channel_id=1, source_target_pairs={{1,0},{2,1},{3,2},{5,4},{6,5},{7,6},{9,8},{10,9},{11,10},{13,12},{... | collective-permute-start | bytes 5898248 | tf_op jit(solution)/shard_map/ppermute | solution.py:23
  297.4 291.6 %copy-start.3 = (s32[1024,16]{0,1:T(8,128)S(1)}, s32[1024,16]{0,1:T(8,128)}, u32[]{:S(2)}) copy-start(s32[1024,16]{0,1:T(8,128)} %param.10) | copy-start | bytes 196612
  297.5 291.5 %all-reduce.6.cloned.1.call-start = ((), (), s32[]{:S(2)}) async-start(), calls=%async_computation.2 | async-start | bytes 8388608 | tf_op jit(solution)/shard_map/psum | solution.py:11
  662.2 18.9 %copy-start.1 = (f32[8,31]{1,0:T(8,128)S(1)}, f32[8,31]{1,0:T(8,128)}, u32[]{:S(2)}) copy-start(f32[8,31]{1,0:T(8,128)} %param.9) | copy-start | bytes 2980
Sparse Core Ops, SparseCore 0:
  297.6 193.4 all-reduce.3
  493.4 95.5 all-reduce.5
